TPU v7x, 512 devices: a whole 4x8x8 slice. The times are simulated.
512 devices in a mesh: ctx: 32 (over y, x), mem: 16 (over z, core).
Axes of the slice: x: 4, y: 8, z: 8, core: 2. Of those that a mesh axis runs over, the one named last changes fastest.
Arguments:
- queries: bfloat16 [65536, 1024], P(('ctx', 'mem')), may hold values from -6 to 6
- key_vectors: bfloat16 [65536, 1024], P(('ctx', 'mem')), may hold values from -30 to 30
- value_vectors: bfloat16 [65536, 1024], P(('ctx', 'mem')), may hold values from -30 to 30
- log_decay: bfloat16 [65536, 16], P(('ctx', 'mem')), may hold values from -1 to 0
- routes: int32 [65536, 2], P(('ctx', 'mem')), may hold values from 0 to 15, all different within a row; in each aligned block of 128 rows (0 to 127, 128 to 255, ...) at most 24 rows name the same one
- route_weight: float32 [65536, 2], P(('ctx', 'mem')), may hold values from 0.2 to 1
- out_gain: float32 [1024], replicated, may hold values from 0.5 to 1.5
Outputs:
- mixed_out: bfloat16 [65536, 1024], P(('ctx', 'mem'))
Inputs may be any that keep to these rules, and one draw needn't show every extreme that they name: `routes`: each token names 2 different memories; among the 128 tokens of one device (aligned blocks) no memory is named more than 24 times, and in every draw some memory is named exactly 24 times.
All inputs are finite; a program needn't handle non-finite values.
Results may differ from a plain program's by a relative error of at most 0.0046.
Values may be sent and summed in bfloat16 or wider, within the bound.
No kernel may reach another device: no remote copies, remote signals or barrier semaphores. Data moves between devices by JAX's collectives and lax.ppermute only.
A program may use at most 128 MiB of HBM per device.

v0:
```python
import jax
import jax.numpy as jnp
from jax import lax
from jax.sharding import PartitionSpec as P

SBLK = 256


precise = lax.Precision.HIGHEST


def carried_in(array, axis, combine, identity):
    peers, place = (lax.axis_size(axis), lax.axis_index(axis))
    everything = jax.tree.map(lambda part: lax.all_gather(part, axis), array)
    start = jax.tree.map(
        lambda part, zero: jnp.broadcast_to(jnp.asarray(zero, part.dtype), part.shape),
        array,
        identity,
    )

    def turn(k, before):
        reached = k < place
        new = combine(before, jax.tree.map(lambda part: part[k], everything))
        return jax.tree.map(lambda a, b: jnp.where(reached, a, b), new, before)

    return lax.fori_loop(0, peers, turn, start)


def block_run(query_blk, key_blk, value_blk, decay_blk):
    head_count = query_blk.shape[2]
    head_size = query_blk.shape[3]

    def advance(carry, pieces):
        state, offset = carry
        query_now, key_now, value_now, decay_now = pieces
        cumul = jnp.cumsum(decay_now, axis=0)
        store_slots_list = jnp.arange(query_now.shape[0], dtype=jnp.int32)
        causal = (store_slots_list[:, None] >= store_slots_list[None, :])[None]
        spread = jnp.transpose(cumul)[:, :, None] - jnp.transpose(cumul)[:, None, :]
        factor = jnp.where(causal, jnp.exp(jnp.where(causal, spread, 0.0)), 0.0)
        scores = jnp.einsum("lhd,shd->hls", query_now, key_now, preferred_element_type=jnp.float32)
        weights = (scores * factor).astype(jnp.bfloat16)
        inner = jnp.einsum("hls,shd->lhd", weights, value_now, preferred_element_type=jnp.float32)
        query_wide = query_now.astype(jnp.float32)
        outer = jnp.einsum(
            "lhd,hde->lhe", query_wide * jnp.exp(cumul)[:, :, None], state, precision=precise
        )
        lifted = query_wide * jnp.exp(cumul + offset[None, :])[:, :, None]
        last = cumul[-1]
        faded = key_now.astype(jnp.float32) * jnp.exp(last[None, :] - cumul)[:, :, None]
        fresh = jnp.einsum("lhd,lhe->hde", faded, value_now.astype(jnp.float32), precision=precise)
        state = jnp.exp(last)[:, None, None] * state + fresh
        return ((state, offset + last), (inner + outer, lifted))

    start = (
        jnp.zeros((head_count, head_size, head_size), jnp.float32),
        jnp.zeros((head_count,), jnp.float32),
    )
    (state, offset), (outputs, lifted) = lax.scan(
        advance, start, (query_blk, key_blk, value_blk, decay_blk)
    )
    return (outputs, lifted, state, offset)


def link(earlier, later):
    early_fade, early_state = earlier
    late_fade, late_state = later
    return (early_fade * late_fade, late_fade * early_state + late_state)


def normed(combined, gains):
    scale = lax.rsqrt(jnp.mean(combined * combined, axis=-1, keepdims=True) + 1e-06)
    return (combined * scale * gains).astype(jnp.bfloat16)


def on_device(queries, key_vectors, value_vectors, log_decay, routes, route_weight, out_gain):
    mem_count = lax.axis_size("mem")
    tok_count = queries.shape[0]
    head_count = log_decay.shape[1]
    feat_width = queries.shape[1]
    head_size = feat_width // head_count
    top_count = routes.shape[1]
    capacity = (3 * tok_count * top_count + 2 * mem_count - 1) // (2 * mem_count)
    query_heads = queries.reshape(tok_count, head_count, head_size)
    key_heads = key_vectors.reshape(tok_count, head_count, head_size)
    value_heads = value_vectors.reshape(tok_count, head_count, head_size)
    shared_q, shared_k, shared_v, shared_g = (
        lax.all_to_all(query_heads, "mem", split_axis=1, concat_axis=0, tiled=True),
        lax.all_to_all(key_heads, "mem", split_axis=1, concat_axis=0, tiled=True),
        lax.all_to_all(value_heads, "mem", split_axis=1, concat_axis=0, tiled=True),
        lax.all_to_all(log_decay, "mem", split_axis=1, concat_axis=0, tiled=True),
    )
    group_rows = shared_q.shape[0]
    local_heads = shared_q.shape[1]
    block_count = group_rows // SBLK

    def blocked(array):
        return array.reshape((block_count, SBLK) + array.shape[1:])

    decay_wide = shared_g.astype(jnp.float32)
    shared_zero, shared_lift, shared_state, shared_offset = block_run(
        blocked(shared_q), blocked(shared_k), blocked(shared_v), blocked(decay_wide)
    )
    mem_ids = jnp.arange(mem_count, dtype=jnp.int32)
    shared_fade = jnp.exp(shared_offset)[:, None, None]
    shared_prefix = carried_in(
        (shared_fade, shared_state),
        "ctx",
        link,
        (jnp.ones_like(shared_fade), jnp.zeros_like(shared_state)),
    )
    shared_out = shared_zero + jnp.einsum(
        "nlhd,hde->nlhe", shared_lift, shared_prefix[1], precision=precise
    )
    shared_out = shared_out.astype(jnp.bfloat16).reshape(group_rows, local_heads, head_size)
    shared_back = lax.all_to_all(shared_out, "mem", split_axis=0, concat_axis=1, tiled=True)
    member = routes[:, :, None] == mem_ids[None, None, :]
    assign = jnp.sum(member.astype(jnp.int32), axis=1)
    ranked = jnp.cumsum(assign, axis=0) - assign
    slot_ids = jnp.arange(capacity, dtype=jnp.int32)
    at_slot = ranked[:, :, None] == slot_ids[None, None, :]
    placing = (at_slot & (assign[:, :, None] == 1)).astype(jnp.bfloat16)

    def dispatched(array):
        moved = jnp.einsum("tmc,tf->mcf", placing, array, preferred_element_type=jnp.float32)
        return moved.astype(jnp.bfloat16)

    send_q = dispatched(queries).reshape(mem_count, capacity, head_count, head_size)
    send_k = dispatched(key_vectors).reshape(mem_count, capacity, head_count, head_size)
    send_v = dispatched(value_vectors).reshape(mem_count, capacity, head_count, head_size)
    send_g = dispatched(log_decay)
    own_q = lax.all_to_all(send_q, "mem", split_axis=0, concat_axis=0, tiled=True)
    own_k = lax.all_to_all(send_k, "mem", split_axis=0, concat_axis=0, tiled=True)
    own_v = lax.all_to_all(send_v, "mem", split_axis=0, concat_axis=0, tiled=True)
    own_g = lax.all_to_all(send_g, "mem", split_axis=0, concat_axis=0, tiled=True)
    sources = own_q.shape[0]
    item_heads = own_q.shape[2]
    span = SBLK // tok_count * capacity
    slot_total = sources * capacity

    def folded(array):
        return array.reshape((slot_total // span, span) + array.shape[2:])

    zero_out, lifted, state, offset = block_run(
        folded(own_q), folded(own_k), folded(own_v), folded(own_g.astype(jnp.float32))
    )
    routed_zero = zero_out.reshape(slot_total, item_heads, head_size)
    routed_lift = lifted.reshape(slot_total, item_heads, head_size)
    routed_state = jnp.moveaxis(state, 0, 1)
    routed_fade = jnp.exp(offset)[None, :, None]
    routed_prefix = carried_in(
        (routed_fade, routed_state),
        "ctx",
        link,
        (jnp.ones_like(routed_fade), jnp.zeros_like(routed_state)),
    )
    routed_out = routed_zero + jnp.einsum(
        "lhd,dhe->lhe", routed_lift, routed_prefix[1], precision=precise
    )
    routed_out = routed_out.astype(jnp.bfloat16).reshape(mem_count, capacity, feat_width)
    returned = lax.all_to_all(routed_out, "mem", split_axis=0, concat_axis=0, tiled=True)
    combined = shared_back.astype(jnp.float32)
    for pick_index in range(top_count):
        chosen = (routes[:, pick_index][:, None] == mem_ids[None, :])[:, :, None] & at_slot
        picked = jnp.einsum(
            "tmc,mcf->tf", chosen.astype(jnp.bfloat16), returned, preferred_element_type=jnp.float32
        )
        combined = combined + route_weight[:, pick_index][:, None, None] * picked.reshape(
            tok_count, head_count, head_size
        )
    result = normed(combined, out_gain.reshape(head_count, head_size))
    return result.reshape(tok_count, feat_width)


def solution(mesh):
    return jax.shard_map(
        on_device,
        mesh=mesh,
        in_specs=(
            P(("ctx", "mem"), None),
            P(("ctx", "mem"), None),
            P(("ctx", "mem"), None),
            P(("ctx", "mem"), None),
            P(("ctx", "mem"), None),
            P(("ctx", "mem"), None),
            P(),
        ),
        out_specs=P(("ctx", "mem"), None),
        check_vma=False,
    )
```

profile of v0, /device:TPU:1, one launch (start us, length us, event | category | flops | bytes accessed | tf_op | source)
XLA Modules:
  0.0 585.5 jit_solution(7565563351947278117)
XLA Ops:
  7.9 11.8 %all-to-all-start = ((bf16[128,16,1]{0,2,1:T(2,128)(2,1)}), bf16[128,16,1]{0,2,1:T(2,128)(2,1)S(1)}, u32[]{:S(2)}, u32[]{:S(2)}) async-start(bf16[128,16,1]{0,2,1:T(2,128)(2,1)} %copy.198), calls=%async_computation | async-start | bytes 16384 | tf_op jit(solution)/shard_map/all_to_all | solution.py:91
  22.5 4.2 all-to-all-done
  26.7 3.9 all-to-all-start.5
  32.5 5.5 all-to-all-done.5
  38.0 3.7 all-to-all-start.1
  42.6 10.9 %all-to-all-done.1 = bf16[128,16,64]{0,2,1:T(8,128)(2,1)S(1)} async-done(((bf16[128,16,64]{0,2,1:T(8,128)(2,1)}), bf16[128,16,64]{0,2,1:T(8,128)(2,1)S(1)}, u32[]{:S(2)}, u32[]{:S(2)}) %all-to-all-start.1) | async-done | bytes 262176 | tf_op jit(solution)/shard_map/all_to_all | solution.py:89
  53.5 3.4 all-to-all-start.2
  57.7 10.1 %all-to-all-done.2 = bf16[128,16,64]{0,2,1:T(8,128)(2,1)S(1)} async-done(((bf16[128,16,64]{0,2,1:T(8,128)(2,1)}), bf16[128,16,64]{0,2,1:T(8,128)(2,1)S(1)}, u32[]{:S(2)}, u32[]{:S(2)}) %all-to-all-start.2) | async-done | bytes 262176 | tf_op jit(solution)/shard_map/all_to_all | solution.py:90
  67.8 3.4 all-to-all-start.3
  74.6 8.4 %all-to-all-done.3 = bf16[128,16,64]{0,2,1:T(8,128)(2,1)S(1)} async-done(((bf16[128,16,64]{0,2,1:T(8,128)(2,1)}), bf16[128,16,64]{0,2,1:T(8,128)(2,1)S(1)}, u32[]{:S(2)}, u32[]{:S(2)}) %all-to-all-start.3) | async-done | bytes 262176 | tf_op jit(solution)/shard_map/all_to_all | solution.py:88
  83.0 3.5 all-to-all-start.6
  92.2 16.2 %all-to-all-done.6 = bf16[16,2,12288]{2,1,0:T(2,128)(2,1)S(1)} async-done(((bf16[16,2,12288]{2,1,0:T(2,128)(2,1)}), bf16[16,2,12288]{2,1,0:T(2,128)(2,1)S(1)}, u32[]{:S(2)}, u32[]{:S(2)}) %all-to-all-start.6) | async-done | bytes 786464 | tf_op jit(solution)/shard_map/all_to_all | solution.py:133
  108.3 4.2 all-to-all-start.7
  118.2 16.2 %all-to-all-done.7 = bf16[16,2,12288]{2,1,0:T(2,128)(2,1)} async-done(((bf16[16,2,12288]{2,1,0:T(2,128)(2,1)}), bf16[16,2,12288]{2,1,0:T(2,128)(2,1)}, u32[]{:S(2)}, u32[]{:S(2)}) %all-to-all-start.7) | async-done | bytes 786464 | tf_op jit(solution)/shard_map/all_to_all | solution.py:134
  134.5 3.5 all-to-all-start.8
  152.1 3.8 reshape.582
  155.9 4.3 all-to-all-done.8
  162.2 54.3 %while.64 = (s32[]{:T(128)}, f32[16,64,64]{2,1,0:T(8,128)S(1)}, f32[16]{0:T(128)S(1)}, f32[8,48,16,64]{3,1,2,0:T(8,128)}, f32[8,48,16,64]{3,1,2,0:T(8,128)}, /*i...) while((s32[]{:T(128)}, f32[16,64,64]{2,1,0:T(8,128)S(1)}, ...), condition=%wide.region_10.11_spmd.clone, body=%wide.region_8.10_spmd.clone.sunk | while | flops 85765152 | bytes 3819553 | solution.py:59
  217.3 54.5 %while.62 = (s32[]{:T(128)}, f32[1,64,64]{2,1,0:T(8,128)S(1)}, f32[1]{0:T(128)}, f32[8,256,1,64]{1,3,2,0:T(8,128)}, f32[8,256,1,64]{1,3,2,0:T(8,128)}, /*index=5...) while((s32[]{:T(128)}, f32[1,64,64]{2,1,0:T(8,128)S(1)}, ...), condition=%wide.region_3.4_spmd.clone, body=%wide.region_0.3_spmd.clone.sunk | while | flops 42500616 | bytes 578834 | solution.py:59
  272.5 47.5 %all-gather.1 = f32[32,64,64]{2,1,0:T(8,128)S(1)} all-gather(f32[1,64,64]{2,1,0:T(8,128)S(1)} %get-tuple-element.295), channel_id=3, replica_groups=mesh['ctx'=32,'mem'=16] {'ctx'}, dimensions={0}, use_global_device_ids=true | all-gather | bytes 540672 | tf_op jit(solution)/shard_map/all_gather | solution.py:14
  320.0 5.0 copy.224
  325.0 3.6 reshape.528
  328.6 5.0 copy.227
  333.6 4.6 reshape.529
  338.2 59.6 %all-reduce.2 = (f32[512]{0:T(512)S(1)}, f32[32]{0:T(128)S(1)}) all-reduce(f32[512]{0:T(512)S(1)} %exponential_dynamic-update-slice_fusion, f32[32]{0:T(128)S(1)} %exponential_dynamic-update-slice_fusion.1), channel_id=4, replica_groups=mesh['ctx'=32,'mem'=16] {'ctx'}, use_global_device_ids=true, to_apply=%add.1 | all-reduce | flops 544 | bytes 4352
  397.9 40.4 %while.63 = (s32[]{:T(128)}, f32[1,64,64]{2,1,0:T(8,128)S(1)}, s32[]{:T(128)}, f32[32,1,1,1]{0,3,2,1:T(1,128)S(1)}, f32[32,1,64,64]{3,2,1,0:T(8,128)S(1)}, /*index=5*/s32[]{:T(128)}, s32[]{:T(128)}) while((s32[]{:T(128)}, f32[1,64,64]{2,1,0:T(8,128)S(1)}, s32[]{:T(128)}, f32[32,1,1,1]{0,3,2,1:T(1,128)S(1)}, ...), condition=%wide.region_5.6_spmd.clone, body=%wide.region_4.5_spmd.clone.sunk | while | flops 16388 | bytes 49277 | solution.py:26
  444.9 12.3 %reduce.2 = bf16[2048,64]{1,0:T(8,128)(2,1)} reduce(bf16[2048,1,64]{2,1,0:T(2,128)(2,1)S(1)} %reshape.575, bf16[]{:T(256)} %broadcast.219), dimensions={1}, to_apply=%reshape.575.reduce_sub_computation | reduce | bytes 524290 | tf_op jit(solution)/shard_map/reshape | solution.py:115
  459.3 23.7 %all-to-all-start.4 = ((bf16[16,2,4096]{2,1,0:T(2,128)(2,1)}), bf16[16,2,4096]{2,1,0:T(2,128)(2,1)S(1)}, u32[]{:S(2)}, u32[]{:S(2)}) async-start(bf16[16,2,4096]{2,1,0:T(2,128)(2,1)} %reshape.585), calls=%async_computation.4 | async-start | bytes 524288 | tf_op jit(solution)/shard_map/all_to_all | solution.py:116
  483.1 17.7 %copy.225 = f32[2048,16,64]{2,1,0:T(8,128)} copy(f32[2048,16,64]{2,0,1:T(8,128)} %all-gather.6.cloned.1.call-done) | data formatting | bytes 16777216 | tf_op jit(solution)/shard_map/all_gather | solution.py:14
  500.8 38.8 %while.65 = (s32[]{:T(128)}, f32[64,16,64]{2,1,0:T(8,128)S(1)}, s32[]{:T(128)}, f32[32,1,16,1]{2,3,1,0:T(1,128)S(1)}, f32[32,64,16,64]{3,2,1,0:T(8,128)}, /*index=5*/s32[]{:T(128)}, s32[]{:T(128)}) while((s32[]{:T(128)}, f32[64,16,64]{2,1,0:T(8,128)S(1)}, s32[]{:T(128)}, f32[32,1,16,1]{2,3,1,0:T(1,128)S(1)}, ...), condition=%wide.region_12.13_spmd.clone, body=%wide.region_11.12_spmd.clone.sunk | while | flops 262148 | bytes 786737 | solution.py:26
  545.8 7.2 %all-to-all-start.9 = ((bf16[16,24,1024]{2,1,0:T(8,128)(2,1)}), bf16[16,24,1024]{2,1,0:T(8,128)(2,1)S(1)}, u32[]{:S(2)}, u32[]{:S(2)}) async-start(bf16[16,24,1024]{2,1,0:T(8,128)(2,1)} %reshape.530), calls=%async_computation.9 | async-start | bytes 1572864 | tf_op jit(solution)/shard_map/all_to_all | solution.py:161
  554.9 20.9 %all-to-all-done.9 = bf16[16,24,1024]{2,1,0:T(8,128)(2,1)S(1)} async-done(((bf16[16,24,1024]{2,1,0:T(8,128)(2,1)}), bf16[16,24,1024]{2,1,0:T(8,128)(2,1)S(1)}, u32[]{:S(2)}, u32[]{:S(2)}) %all-to-all-start.9) | async-done | bytes 786464 | tf_op jit(solution)/shard_map/all_to_all | solution.py:161
  (470 shorter events, 234.8 us)
Async XLA Ops:
  6.5 35.2 %copy-start.4 = (bf16[128,1024]{1,0:T(8,128)(2,1)S(1)}, bf16[128,1024]{1,0:T(8,128)(2,1)}, u32[]{:S(2)}) copy-start(bf16[128,1024]{1,0:T(8,128)(2,1)} %param.17) | copy-start | bytes 786436
  6.5 50.4 %copy-start.6 = (bf16[128,1024]{1,0:T(8,128)(2,1)S(1)}, bf16[128,1024]{1,0:T(8,128)(2,1)}, u32[]{:S(2)}) copy-start(bf16[128,1024]{1,0:T(8,128)(2,1)} %param.15) | copy-start | bytes 786436
  7.9 18.8 %all-to-all-start = ((bf16[128,16,1]{0,2,1:T(2,128)(2,1)}), bf16[128,16,1]{0,2,1:T(2,128)(2,1)S(1)}, u32[]{:S(2)}, u32[]{:S(2)}) async-start(bf16[128,16,1]{0,2,1:T(2,128)(2,1)} %copy.198), calls=%async_computation | async-start | bytes 16384 | tf_op jit(solution)/shard_map/all_to_all | solution.py:91
  26.7 11.3 %all-to-all-start.5 = ((bf16[16,2,192]{2,1,0:T(2,128)(2,1)}), bf16[16,2,192]{2,1,0:T(2,128)(2,1)S(1)}, u32[]{:S(2)}, u32[]{:S(2)}) async-start(bf16[16,2,192]{2,1,0:T(2,128)(2,1)} %reshape.577), calls=%async_computation.5 | async-start | bytes 32768 | tf_op jit(solution)/shard_map/all_to_all | solution.py:135
  30.6 40.7 %copy-start.3 = (bf16[128,1024]{1,0:T(8,128)(2,1)S(1)}, bf16[128,1024]{1,0:T(8,128)(2,1)}, u32[]{:S(2)}) copy-start(bf16[128,1024]{1,0:T(8,128)(2,1)} %param.16) | copy-start | bytes 786436
  38.0 15.5 %all-to-all-start.1 = ((bf16[128,16,64]{0,2,1:T(8,128)(2,1)}), bf16[128,16,64]{0,2,1:T(8,128)(2,1)S(1)}, u32[]{:S(2)}, u32[]{:S(2)}) async-start(bf16[128,16,64]{0,2,1:T(8,128)(2,1)} %bitcast.3), calls=%async_computation.1 | async-start | bytes 524288 | tf_op jit(solution)/shard_map/all_to_all | solution.py:89
  53.5 14.4 %all-to-all-start.2 = ((bf16[128,16,64]{0,2,1:T(8,128)(2,1)}), bf16[128,16,64]{0,2,1:T(8,128)(2,1)S(1)}, u32[]{:S(2)}, u32[]{:S(2)}) async-start(bf16[128,16,64]{0,2,1:T(8,128)(2,1)} %bitcast.6), calls=%async_computation.2 | async-start | bytes 524288 | tf_op jit(solution)/shard_map/all_to_all | solution.py:90
  67.8 15.2 %all-to-all-start.3 = ((bf16[128,16,64]{0,2,1:T(8,128)(2,1)}), bf16[128,16,64]{0,2,1:T(8,128)(2,1)S(1)}, u32[]{:S(2)}, u32[]{:S(2)}) async-start(bf16[128,16,64]{0,2,1:T(8,128)(2,1)} %bitcast.9), calls=%async_computation.3 | async-start | bytes 524288 | tf_op jit(solution)/shard_map/all_to_all | solution.py:88
  72.7 13.9 %copy-start.5 = (bf16[128,1024]{1,0:T(8,128)(2,1)S(1)}, bf16[128,1024]{1,0:T(8,128)(2,1)}, u32[]{:S(2)}) copy-start(bf16[128,1024]{1,0:T(8,128)(2,1)} %param.17) | copy-start | bytes 786436
  83.0 7.3 %copy-start.1 = (bf16[128,16,64]{0,2,1:T(8,128)(2,1)}, bf16[128,16,64]{0,2,1:T(8,128)(2,1)S(1)}, u32[]{:S(2)}) copy-start(bf16[128,16,64]{0,2,1:T(8,128)(2,1)S(1)} %all-to-all-done.3) | copy-start | bytes 786436
  83.0 25.3 %all-to-all-start.6 = ((bf16[16,2,12288]{2,1,0:T(2,128)(2,1)}), bf16[16,2,12288]{2,1,0:T(2,128)(2,1)S(1)}, u32[]{:S(2)}, u32[]{:S(2)}) async-start(bf16[16,2,12288]{2,1,0:T(2,128)(2,1)} %reshape.579), calls=%async_computation.6 | async-start | bytes 1572864 | tf_op jit(solution)/shard_map/all_to_all | solution.py:133
  90.3 22.2 %copy-start.7 = (bf16[128,1024]{1,0:T(8,128)(2,1)S(1)}, bf16[128,1024]{1,0:T(8,128)(2,1)}, u32[]{:S(2)}) copy-start(bf16[128,1024]{1,0:T(8,128)(2,1)} %param.15) | copy-start | bytes 786436
  108.3 26.1 %all-to-all-start.7 = ((bf16[16,2,12288]{2,1,0:T(2,128)(2,1)}), bf16[16,2,12288]{2,1,0:T(2,128)(2,1)}, u32[]{:S(2)}, u32[]{:S(2)}) async-start(bf16[16,2,12288]{2,1,0:T(2,128)(2,1)} %reshape.581), calls=%async_computation.7 | async-start | bytes 1572864 | tf_op jit(solution)/shard_map/all_to_all | solution.py:134
  134.5 25.8 %all-to-all-start.8 = ((bf16[16,2,12288]{2,1,0:T(2,128)(2,1)}), bf16[16,2,12288]{2,1,0:T(2,128)(2,1)S(1)}, u32[]{:S(2)}, u32[]{:S(2)}) async-start(bf16[16,2,12288]{2,1,0:T(2,128)(2,1)} %reshape.583), calls=%async_computation.8 | async-start | bytes 1572864 | tf_op jit(solution)/shard_map/all_to_all | solution.py:132
  138.0 345.1 %all-gather.6.cloned.1.call-start = ((), (), s32[]{:S(2)}) async-start(), calls=%async_computation.10 | async-start | bytes 17301504 | tf_op jit(solution)/shard_map/all_gather | solution.py:14
  142.1 6.2 %copy-start.2 = (bf16[128,16,64]{0,2,1:T(8,128)(2,1)S(1)}, bf16[128,16,64]{0,2,1:T(8,128)(2,1)}, u32[]{:S(2)}) copy-start(bf16[128,16,64]{0,2,1:T(8,128)(2,1)} %copy-done.1) | copy-start | bytes 786436
  216.4 0.8 copy-start
  459.3 86.5 %all-to-all-start.4 = ((bf16[16,2,4096]{2,1,0:T(2,128)(2,1)}), bf16[16,2,4096]{2,1,0:T(2,128)(2,1)S(1)}, u32[]{:S(2)}, u32[]{:S(2)}) async-start(bf16[16,2,4096]{2,1,0:T(2,128)(2,1)} %reshape.585), calls=%async_computation.4 | async-start | bytes 524288 | tf_op jit(solution)/shard_map/all_to_all | solution.py:116
  543.9 9.1 %copy-start.9 = (s32[128,2]{0,1:T(2,128)S(1)}, s32[128,2]{0,1:T(2,128)}, u32[]{:S(2)}) copy-start(s32[128,2]{0,1:T(2,128)} %param.19) | copy-start | bytes 3076
  543.9 9.1 %copy-start.10 = (f32[128,2]{0,1:T(2,128)S(1)}, f32[128,2]{0,1:T(2,128)}, u32[]{:S(2)}) copy-start(f32[128,2]{0,1:T(2,128)} %param.20) | copy-start | bytes 3076
  545.8 29.9 %all-to-all-start.9 = ((bf16[16,24,1024]{2,1,0:T(8,128)(2,1)}), bf16[16,24,1024]{2,1,0:T(8,128)(2,1)S(1)}, u32[]{:S(2)}, u32[]{:S(2)}) async-start(bf16[16,24,1024]{2,1,0:T(8,128)(2,1)} %reshape.530), calls=%async_computation.9 | async-start | bytes 1572864 | tf_op jit(solution)/shard_map/all_to_all | solution.py:161
  576.9 0.9 copy-start.8
Sparse Core Ops, SparseCore 0:
  217.4 145.6 all-gather.5
where the time goes:
time: 591 us; the launch traced here: 585 us
  local copies, waits for them, and re-layouts  140 us (24%)
  blocking collectives  107 us (18%)
  waiting for transfers between devices  96.8 us (16%)
  other arithmetic  91.5 us (15%)
  starting transfers between devices  68.7 us (12%)
  matrix products  54.6 us (9%)
  between operations  14.5 us (2%)
  loops' own time  11.9 us (2%)
    unnamed x1, blocking collectives  59.6 us
    select_n x64, other arithmetic, turn(): return jax.tree.map(lambda a, b: jnp.where(reached, a, b), new, before)  58.5 us
    all_gather x1, blocking collectives, carried_in(): everything = jax.tree.map(lambda part: lax.all_gather(part, axis), array)  47.5 us
    unnamed x45, local copies, waits for them, and re-layouts  27.7 us
    all_to_all x1, starting transfers between devices, on_device(): lax.all_to_all(shared_out, 'mem', split_axis=0, concat_axis=1, tiled=True)  23.7 us
    all_to_all x1, waiting for transfers between devices, on_device(): lax.all_to_all(routed_out, 'mem', split_axis=0, concat_axis=0, tiled=True)  20.9 us
    dynamic_slice x32, local copies, waits for them, and re-layouts, turn(): new = combine(before, jax.tree.map(lambda part: part[k], everything))  18.7 us
    dot_general x16, matrix products, advance(): jnp.einsum('hls,shd->lhd', weights, value_now, preferred_element_type=jnp...  18.2 us
  transfers between devices with their start and end apart: 11, of which 9 were waited for; matrix products, arithmetic and copies ran while one was open for 39% of the time, Pallas kernels for 0%

commit v1 on v0

v1 whole, which is shorter than its diff:
```python
import functools

import jax
import jax.numpy as jnp
from jax import lax
from jax.experimental import pallas as pl
from jax.experimental.pallas import tpu as pltpu
from jax.sharding import PartitionSpec as P

MEMS = 16
SETS = 17
ROWS = 24
EXTRA = 16
BF = jnp.bfloat16
F32 = jnp.float32


def iota(shape, dim):
    return lax.broadcasted_iota(jnp.int32, shape, dim)


def dot(a, b, ca, cb):
    return lax.dot_general(a, b, (((ca,), (cb,)), ((), ())), preferred_element_type=F32)


def halves(x):
    high = x.astype(BF)
    return high, (x - high.astype(F32)).astype(BF)


def call(body, out_shape, *args, scratch=(), name=None):
    return pl.pallas_call(
        body,
        out_shape=out_shape,
        scratch_shapes=list(scratch),
        name=name,
        compiler_params=pltpu.CompilerParams(vmem_limit_bytes=48 << 20),
    )(*args)


def spread_body(k_ref, v_ref, g_ref, r_ref, w_ref, out_ref):
    width = k_ref.shape[0]
    head_size = k_ref.shape[1] // out_ref.shape[0]
    per = 128 // head_size
    eye = (iota((128, 128), 0) == iota((128, 128), 1)).astype(BF)
    routes = r_ref[...].astype(F32)
    weights = w_ref[...]
    high = weights.astype(BF).astype(F32)
    low = weights - high
    rows = iota((EXTRA, width), 0)
    common = jnp.zeros((EXTRA, width), F32)
    for place, line in enumerate(
        (routes[0:1], routes[1:2], high[0:1], high[1:2], low[0:1], low[1:2])
    ):
        common = jnp.where(rows == place + 1, line, common)
    decay = g_ref[...].astype(F32)
    for chunk in range(k_ref.shape[1] // 128):
        for base, ref in ((0, k_ref), (head_size, v_ref)):
            turned = dot(eye, ref[:, chunk * 128 : (chunk + 1) * 128], 1, 1).astype(BF)
            for part in range(per):
                out_ref[chunk * per + part, base : base + head_size, :] = turned[
                    part * head_size : (part + 1) * head_size, :
                ]
    for head in range(out_ref.shape[0]):
        out_ref[head, 2 * head_size : 2 * head_size + EXTRA, :] = jnp.where(
            rows == 0, decay[head : head + 1], common
        ).astype(BF)


def turn_body(q_ref, out_ref):
    head_size = out_ref.shape[1]
    per = 128 // head_size
    eye = (iota((128, 128), 0) == iota((128, 128), 1)).astype(BF)
    for chunk in range(q_ref.shape[1] // 128):
        turned = dot(eye, q_ref[:, chunk * 128 : (chunk + 1) * 128], 1, 1).astype(BF)
        for part in range(per):
            out_ref[chunk * per + part] = turned[part * head_size : (part + 1) * head_size, :]


def back_body(x_ref, out_ref):
    head_size = x_ref.shape[1]
    per = 128 // head_size
    eye = (iota((128, 128), 0) == iota((128, 128), 1)).astype(BF)
    for chunk in range(out_ref.shape[1] // 128):
        slab = x_ref[chunk * per : (chunk + 1) * per].reshape(128, 128)
        out_ref[:, chunk * 128 : (chunk + 1) * 128] = dot(eye, slab, 1, 1).astype(BF)


def tables(extra):
    width = extra.shape[1]
    ids = iota((ROWS, width), 0).astype(F32)
    first, second = extra[1:2], extra[2:3]
    member = (ids == first) | (ids == second) | (ids == float(MEMS))
    upper = (iota((width, width), 0) <= iota((width, width), 1)).astype(BF)
    decay = jnp.where(member, extra[0:1], 0.0).astype(BF)
    cumul = dot(decay, upper, 1, 0)
    return member, cumul, cumul[:, width - 1 : width]


def read_weights(extra):
    width = extra.shape[1]
    ids = iota((ROWS, width), 0).astype(F32)
    zero = jnp.zeros((ROWS, width), F32)
    return (
        jnp.where(ids == extra[1:2], extra[3:4] + extra[5:6], zero)
        + jnp.where(ids == extra[2:3], extra[4:5] + extra[6:7], zero)
        + jnp.where(ids == float(MEMS), 1.0, zero)
    )


def added(kv_ref, block, reach, scale, out):
    head_size = (kv_ref.shape[1] - EXTRA) // 2
    keys = kv_ref[block, 0:head_size, :]
    values = kv_ref[block, head_size : 2 * head_size, :].astype(F32)
    twice = jnp.concatenate([keys, keys], axis=0)
    twice = jnp.concatenate([twice, twice], axis=1)
    for one in range(SETS):
        high, low = halves(values * reach[one : one + 1])
        fresh = dot(jnp.concatenate([high, low], axis=1), twice, 1, 1)
        out(one, fresh)


def totals_body(pieces, kv_ref, out_ref, state_ref):
    blocks, height, width = kv_ref.shape
    head_size = (height - EXTRA) // 2
    state_ref[...] = jnp.zeros_like(state_ref)

    def step(turn, after):
        block = blocks - 1 - turn
        extra = kv_ref[block, 2 * head_size : height, :].astype(F32)
        member, cumul, total = tables(extra)
        reach = jnp.where(member, jnp.exp(total - cumul + after), 0.0)

        def out(one, fresh):
            state_ref[one] += fresh

        added(kv_ref, block, reach, None, out)
        return after + total

    after = lax.fori_loop(0, blocks, step, jnp.zeros((ROWS, width), F32))
    left = iota((8, width), 1) < head_size
    rows = iota((8, width), 0)
    parts = pieces // MEMS
    lines = head_size // 2 // parts
    plain = after.astype(BF).astype(F32)
    middle = (after - plain).astype(BF).astype(F32)
    rest = after - plain - middle
    for piece in range(pieces):
        one, part = piece // parts, piece % parts
        for base in range(0, lines, 8):
            start = part * 2 * lines + base
            out_ref[piece, base : base + 8, :] = jnp.where(
                left,
                state_ref[one, start : start + 8, :],
                state_ref[one, start + lines : start + lines + 8, :],
            ).astype(out_ref.dtype)
        shared = jnp.where(
            left[0:1],
            state_ref[MEMS, piece : piece + 1, :],
            state_ref[MEMS, piece + head_size // 2 : piece + head_size // 2 + 1, :],
        )
        tail = jnp.where(rows == 0, shared, 0.0)
        for place, line in enumerate(
            (plain[one : one + 1], middle[one : one + 1], rest[one : one + 1],
             plain[MEMS : MEMS + 1], middle[MEMS : MEMS + 1], rest[MEMS : MEMS + 1])
        ):
            tail = jnp.where(rows == place + 1, line, tail)
        out_ref[piece, lines : lines + 8, :] = tail.astype(out_ref.dtype)


def prefix_body(x_ref, out_ref):
    peers, height, width = x_ref.shape
    lines = height - 8
    rows = iota((height, width), 0)
    before = jnp.zeros((height, width), F32)
    for peer in range(peers):
        out_ref[peer] = before.astype(out_ref.dtype)
        if peer < peers - 1:
            own = x_ref[peer].astype(F32)
            routed = own[lines + 1 : lines + 2] + own[lines + 2 : lines + 3] + own[lines + 3 : lines + 4]
            shared = own[lines + 4 : lines + 5] + own[lines + 5 : lines + 6] + own[lines + 6 : lines + 7]
            fade = jnp.exp(jnp.where(rows < lines, routed, shared))
            before = fade * before + own


def local_body(kv_ref, q_ref, out_ref, lift_ref, state_ref):
    blocks, height, width = kv_ref.shape
    head_size = (height - EXTRA) // 2
    state_ref[...] = jnp.zeros_like(state_ref)

    def step(block, offset):
        extra = kv_ref[block, 2 * head_size : height, :].astype(F32)
        member, cumul, total = tables(extra)
        share = read_weights(extra)
        lift_ref[block] = share * jnp.exp(cumul + offset)
        keys = kv_ref[block, 0:head_size, :]
        values = kv_ref[block, head_size : 2 * head_size, :]
        queries = q_ref[block]
        middle = cumul[:, width // 2 - 1 : width // 2]
        write_high, write_low = halves(jnp.where(member, jnp.exp(middle - cumul), 0.0))
        read_high, read_low = halves(share * jnp.exp(cumul - middle))
        factor = dot(
            jnp.concatenate([write_high, write_low, write_high], axis=0),
            jnp.concatenate([read_high, read_high, read_low], axis=0),
            0,
            0,
        )
        causal = iota((width, width), 0) <= iota((width, width), 1)
        scores = dot(keys, queries, 0, 0)
        high, low = halves(jnp.where(causal, scores * factor, 0.0))
        total_out = dot(
            jnp.concatenate([values, values], axis=1), jnp.concatenate([high, low], axis=0), 1, 0
        )
        pair = jnp.concatenate([queries, queries], axis=0)
        lift = share * jnp.exp(cumul)
        left = iota((head_size, 2 * head_size), 1) < head_size
        fade = jnp.exp(total)
        for one in range(SETS):
            high, low = halves(state_ref[one])
            seen = dot(jnp.where(left, high, low), pair, 1, 0)
            total_out = total_out + lift[one : one + 1] * seen
        out_ref[block] = total_out
        reach = jnp.where(member, jnp.exp(total - cumul), 0.0)

        def out(one, fresh):
            state_ref[one] = fade[one : one + 1] * state_ref[one] + fresh

        added(kv_ref, block, reach, fade, out)
        return offset + total

    lax.fori_loop(0, blocks, step, jnp.zeros((ROWS, width), F32))


def finish_body(before_ref, q_ref, local_ref, lift_ref, gain_ref, out_ref, shared_ref):
    pieces = before_ref.shape[0]
    lines = before_ref.shape[1] - 8
    blocks, head_size, width = q_ref.shape
    parts = pieces // MEMS
    half = head_size // 2
    for piece in range(pieces):
        shared_ref[piece : piece + 1, :] = before_ref[piece, lines : lines + 8, :].astype(F32)[0:1]
    gain = gain_ref[...]

    def step(block, carry):
        queries = q_ref[block]
        zero = jnp.zeros_like(queries)
        sides = jnp.concatenate(
            [jnp.concatenate([queries, zero], axis=1), jnp.concatenate([zero, queries], axis=1)],
            axis=0,
        )
        lift = lift_ref[block]
        both = dot(shared_ref[...].astype(BF), sides, 1, 0)
        line = lift[MEMS : MEMS + 1]
        add = jnp.concatenate([both[:, :width], both[:, width:]], axis=0) * line
        groups = [add[2 * lines * part : 2 * lines * (part + 1)] for part in range(parts)]
        for piece in range(pieces):
            one, part = piece // parts, piece % parts
            seen = dot(before_ref[piece, 0:lines, :].astype(BF), sides, 1, 0)
            line = lift[one : one + 1]
            groups[part] = groups[part] + line * jnp.concatenate(
                [seen[:, :width], seen[:, width:]], axis=0
            )
        combined = local_ref[block] + jnp.concatenate(groups, axis=0)
        mean = jnp.sum(combined * combined, axis=0, keepdims=True) * (1.0 / head_size)
        out_ref[block] = (combined * lax.rsqrt(mean + 1e-06) * gain).astype(BF)
        return carry

    lax.fori_loop(0, blocks, step, 0)


def shape(dims, dtype):
    return jax.ShapeDtypeStruct(dims, dtype)


def exchange(x, axis):
    return lax.all_to_all(x, axis, split_axis=0, concat_axis=0, tiled=True)


SEND = BF


def spread(keys, values, decay, routes, weights, heads):
    width = keys.shape[0]
    head_size = keys.shape[1] // heads
    return call(
        spread_body, shape((heads, 2 * head_size + EXTRA, width), BF),
        keys, values, decay.T, routes.T, weights.T, name="spread",
    )


def turn(queries, heads):
    return call(
        turn_body, shape((heads, queries.shape[1] // heads, queries.shape[0]), BF), queries,
        name="turn",
    )


def totals(kv, pieces):
    head_size, width = (kv.shape[1] - EXTRA) // 2, kv.shape[2]
    lines = MEMS * head_size // 2 // pieces
    return call(
        functools.partial(totals_body, pieces), shape((pieces, lines + 8, width), SEND), kv,
        scratch=[pltpu.VMEM((SETS, head_size, width), F32)], name="totals",
    )


def prefix(x):
    return call(prefix_body, shape(x.shape, x.dtype), x, name="prefix")


def local(kv, q):
    blocks, head_size, width = q.shape
    return call(
        local_body,
        (shape((blocks, head_size, width), F32), shape((blocks, ROWS, width), F32)),
        kv, q, scratch=[pltpu.VMEM((SETS, head_size, width), F32)], name="local",
    )


def finish(before, q, inner, lift, gain):
    head_size, width = q.shape[1:]
    return call(
        finish_body, shape(q.shape, BF), before, q, inner, lift, gain,
        scratch=[pltpu.VMEM((head_size // 2, width), F32)], name="finish",
    )


def back(x, tokens, feats):
    return call(back_body, shape((tokens, feats), BF), x, name="back")


def on_device(queries, key_vectors, value_vectors, log_decay, routes, route_weight, out_gain):
    heads = lax.axis_size("mem")
    pieces = lax.axis_size("ctx")
    tokens, feats = queries.shape
    head_size = feats // heads
    kv = exchange(spread(key_vectors, value_vectors, log_decay, routes, route_weight, heads), "mem")
    q = exchange(turn(queries, heads), "mem")
    gathered = exchange(totals(kv, pieces), "ctx")
    inner, lift = local(kv, q)
    before = exchange(prefix(gathered), "ctx")
    mine = lax.dynamic_slice_in_dim(out_gain, lax.axis_index("mem") * head_size, head_size)
    gain = jnp.broadcast_to(mine[:, None], (head_size, tokens))
    done = exchange(finish(before, q, inner, lift, gain), "mem")
    return back(done, tokens, feats)


def solution(mesh):
    rows = P(("ctx", "mem"), None)
    return jax.shard_map(
        on_device,
        mesh=mesh,
        in_specs=(rows, rows, rows, rows, rows, rows, P()),
        out_specs=rows,
        check_vma=False,
    )
```

time: 591 us -> 128 us (0.22)
  local copies, waits for them, and re-layouts: 140 us -> 4.11 us
  other arithmetic: 91.5 us -> 0 us
  waiting for transfers between devices: 96.8 us -> 20.5 us
  blocking collectives: 107 us -> 44.8 us
  matrix products: 54.6 us -> 0 us
  starting transfers between devices: 68.7 us -> 19.1 us
  Pallas kernels: 0 us -> 39.1 us
  between operations: 14.5 us -> 0.07 us
  loops' own time: 11.9 us -> 0 us
    all_to_all x10 -> x3, waiting for transfers between devices: 96.8 us -> 20.5 us  [exchange(): return lax.all_to_all(x, axis, split_axis=0, concat_axis=0, tiled=True)]
    unnamed x1 -> x0, blocking collectives: 59.6 us -> none
    select_n x64 -> x0, other arithmetic: 58.5 us -> none  [turn(): return jax.tree.map(lambda a, b: jnp.where(reached, a, b), new, before)]
    dot_general x56 -> x0, matrix products: 54.6 us -> none  [the longest x16 18.2 us: advance(): jnp.einsum('hls,shd->lhd', weights, value_now, preferred_element_type=jnp...]
    all_to_all x10 -> x3, starting transfers between devices: 68.5 us -> 19.1 us  [exchange(): return lax.all_to_all(x, axis, split_axis=0, concat_axis=0, tiled=True)]
    all_gather x1 -> x0, blocking collectives: 47.5 us -> none  [carried_in(): everything = jax.tree.map(lambda part: lax.all_gather(part, axis), array)]
    all_to_all x0 -> x2, blocking collectives: none -> 44.8 us  [exchange(): return lax.all_to_all(x, axis, split_axis=0, concat_axis=0, tiled=True)]
    pallas_call x0 -> x7, Pallas kernels: none -> 39.1 us  [call(): pl.pallas_call(body, out_shape=out_shape, scratch_shapes=list(scratch), n...]
  transfers between devices with their start and end apart: 11 -> 3, of which waited for: 9 -> 2; matrix products, arithmetic and copies ran while one was open for 39% -> 1% of each run, Pallas kernels for 0% -> 15%
where the time goes in v1:
time: 128 us
  blocking collectives  44.8 us (35%)
  Pallas kernels  39.1 us (31%)
  waiting for transfers between devices  20.5 us (16%)
  starting transfers between devices  19.1 us (15%)
  local copies, waits for them, and re-layouts  4.11 us (3%)
    all_to_all x2, blocking collectives, exchange(): return lax.all_to_all(x, axis, split_axis=0, concat_axis=0, tiled=True)  44.8 us
    pallas_call x7, Pallas kernels, call(): pl.pallas_call(body, out_shape=out_shape, scratch_shapes=list(scratch), n...  39.1 us
    all_to_all x3, waiting for transfers between devices, exchange(): return lax.all_to_all(x, axis, split_axis=0, concat_axis=0, tiled=True)  20.5 us
    all_to_all x3, starting transfers between devices, exchange(): return lax.all_to_all(x, axis, split_axis=0, concat_axis=0, tiled=True)  19.1 us
    unnamed x12, local copies, waits for them, and re-layouts  3.27 us
  transfers between devices with their start and end apart: 3, of which 2 were waited for; matrix products, arithmetic and copies ran while one was open for 1% of the time, Pallas kernels for 15%

profile of v1, /device:TPU:1, one launch (start us, length us, event | category | flops | bytes accessed | tf_op | source)
XLA Modules:
  0.0 127.7 jit_solution(10169786846367832330)
XLA Ops:
  0.0 0.0 copy-start.3
  0.0 0.0 copy-start.4
  0.0 0.7 copy-done.3
  0.7 0.0 copy-done.4
  0.7 0.0 copy-start
  0.7 0.9 copy-done
  1.6 0.0 copy-start.1
  1.6 0.9 copy-done.1
  2.6 0.0 copy-start.5
  2.6 0.7 copy-done.5
  3.3 0.5 spread.1
  3.8 30.5 %all_to_all.25.kv_ref = bf16[16,144,128]{2,1,0:T(8,128)(2,1)S(1)} all-to-all(bf16[16,144,128]{2,1,0:T(8,128)(2,1)S(1)} %spread.1), channel_id=1, replica_groups=mesh['ctx'=32,'mem'=16] {'mem'}, dimensions={0} | all-to-all | bytes 1179648 | tf_op jit(solution)/shard_map/all_to_all | solution.py:276
  34.3 12.2 %totals.1 = bf16[32,24,128]{2,1,0:T(8,128)(2,1)} custom-call(bf16[16,144,128]{2,1,0:T(8,128)(2,1)S(1)} %all_to_all.25.kv_ref), custom_call_target="tpu_custom_call" | custom-call | tf_op jit(solution)/shard_map/totals/pallas_call | solution.py:32
  46.5 0.0 copy-start.2
  46.5 9.8 %all-to-all-start.1 = ((bf16[32,24,128]{2,1,0:T(8,128)(2,1)}), bf16[32,24,128]{2,1,0:T(8,128)(2,1)S(1)}, u32[]{:S(2)}, u32[]{:S(2)}) async-start(bf16[32,24,128]{2,1,0:T(8,128)(2,1)} %totals.1), calls=%async_computation.1 | async-start | bytes 393216 | tf_op jit(solution)/shard_map/all_to_all | solution.py:276
  56.3 0.0 copy-done.2
  56.3 1.0 turn.1
  57.3 9.5 %all-to-all-done.1.x_ref = bf16[32,24,128]{2,1,0:T(8,128)(2,1)S(1)} async-done(((bf16[32,24,128]{2,1,0:T(8,128)(2,1)}), bf16[32,24,128]{2,1,0:T(8,128)(2,1)S(1)}, u32[]{:S(2)}, u32[]{:S(2)}) %all-to-all-start.1) | async-done | bytes 196640 | tf_op jit(solution)/shard_map/all_to_all | solution.py:276
  66.8 5.5 %all-to-all-start.3 = ((bf16[16,64,128]{2,1,0:T(8,128)(2,1)}), bf16[16,64,128]{2,1,0:T(8,128)(2,1)S(1)}, u32[]{:S(2)}, u32[]{:S(2)}) async-start(bf16[16,64,128]{2,1,0:T(8,128)(2,1)} %turn.1), calls=%async_computation.3 | async-start | bytes 524288 | tf_op jit(solution)/shard_map/all_to_all | solution.py:276
  72.3 0.8 prefix.1
  73.0 11.0 %all-to-all-done.3.q_ref = bf16[16,64,128]{2,1,0:T(8,128)(2,1)S(1)} async-done(((bf16[16,64,128]{2,1,0:T(8,128)(2,1)}), bf16[16,64,128]{2,1,0:T(8,128)(2,1)S(1)}, u32[]{:S(2)}, u32[]{:S(2)}) %all-to-all-start.3) | async-done | bytes 262176 | tf_op jit(solution)/shard_map/all_to_all | solution.py:276
  84.0 3.9 %all-to-all-start.2 = ((bf16[32,24,128]{2,1,0:T(8,128)(2,1)}), bf16[32,24,128]{2,1,0:T(8,128)(2,1)S(1)}, u32[]{:S(2)}, u32[]{:S(2)}) async-start(bf16[32,24,128]{2,1,0:T(8,128)(2,1)} %prefix.1), calls=%async_computation.2 | async-start | bytes 393216 | tf_op jit(solution)/shard_map/all_to_all | solution.py:276
  87.9 0.8 dynamic_slice.3
  88.7 16.8 %local.1 = (f32[16,64,128]{2,1,0:T(8,128)S(1)}, f32[16,24,128]{2,1,0:T(8,128)S(1)}) custom-call(bf16[16,144,128]{2,1,0:T(8,128)(2,1)S(1)} %all_to_all.25.kv_ref, bf16[16,64,128]{2,1,0:T(8,128)(2,1)S(1)} %all-to-all-done.3.q_ref), custom_call_target="tpu_custom_call" | custom-call | tf_op jit(solution)/shard_map/local/pallas_call | solution.py:32
  105.5 0.0 all-to-all-done.2.before_ref
  105.5 0.1 broadcast_in_dim.2.gain_ref
  105.6 6.9 %finish.1 = bf16[16,64,128]{2,1,0:T(8,128)(2,1)S(1)} custom-call(bf16[32,24,128]{2,1,0:T(8,128)(2,1)S(1)} %all-to-all-done.2.before_ref, bf16[16,64,128]{2,1,0:T(8,128)(2,1)S(1)} %all-to-all-done.3.q_ref, f32[16,64,128]{2,1,0:T(8,128)S(1)} %get-tuple-element.7.local_ref, f32[16,24,128]{2,1,0:T(8,128)S(1)} %get-tuple-element.8.lift_ref, ...), custom_call_target="tpu_custom_call" | custom-call | tf_op jit(solution)/shard_map/finish/pallas_call | solution.py:32
  112.5 14.2 %all_to_all.26.x_ref = bf16[16,64,128]{2,1,0:T(8,128)(2,1)S(1)} all-to-all(bf16[16,64,128]{2,1,0:T(8,128)(2,1)S(1)} %finish.1), channel_id=1, replica_groups=mesh['ctx'=32,'mem'=16] {'mem'}, dimensions={0} | all-to-all | bytes 524288 | tf_op jit(solution)/shard_map/all_to_all | solution.py:276
  126.7 1.0 back.1
Async XLA Ops:
  0.0 0.7 copy-start.3
  0.0 0.7 copy-start.4
  0.7 0.9 copy-start
  1.6 0.9 copy-start.1
  2.6 0.7 copy-start.5
  46.5 9.8 %copy-start.2 = (bf16[128,1024]{1,0:T(8,128)(2,1)S(1)}, bf16[128,1024]{1,0:T(8,128)(2,1)}, u32[]{:S(2)}) copy-start(bf16[128,1024]{1,0:T(8,128)(2,1)} %q_ref.1) | copy-start | bytes 786436
  46.5 20.4 %all-to-all-start.1 = ((bf16[32,24,128]{2,1,0:T(8,128)(2,1)}), bf16[32,24,128]{2,1,0:T(8,128)(2,1)S(1)}, u32[]{:S(2)}, u32[]{:S(2)}) async-start(bf16[32,24,128]{2,1,0:T(8,128)(2,1)} %totals.1), calls=%async_computation.1 | async-start | bytes 393216 | tf_op jit(solution)/shard_map/all_to_all | solution.py:276
  66.8 17.2 %all-to-all-start.3 = ((bf16[16,64,128]{2,1,0:T(8,128)(2,1)}), bf16[16,64,128]{2,1,0:T(8,128)(2,1)S(1)}, u32[]{:S(2)}, u32[]{:S(2)}) async-start(bf16[16,64,128]{2,1,0:T(8,128)(2,1)} %turn.1), calls=%async_computation.3 | async-start | bytes 524288 | tf_op jit(solution)/shard_map/all_to_all | solution.py:276
  84.0 21.5 %all-to-all-start.2 = ((bf16[32,24,128]{2,1,0:T(8,128)(2,1)}), bf16[32,24,128]{2,1,0:T(8,128)(2,1)S(1)}, u32[]{:S(2)}, u32[]{:S(2)}) async-start(bf16[32,24,128]{2,1,0:T(8,128)(2,1)} %prefix.1), calls=%async_computation.2 | async-start | bytes 393216 | tf_op jit(solution)/shard_map/all_to_all | solution.py:276

commit v2 on v1

v2 whole, which is shorter than its diff:
```python
import functools

import jax
import jax.numpy as jnp
from jax import lax
from jax.experimental import pallas as pl
from jax.experimental.pallas import tpu as pltpu
from jax.sharding import PartitionSpec as P


MEMS = 16
SETS = 17
ROWS = 24
EXTRA = 16
BF = jnp.bfloat16
F32 = jnp.float32


def iota(shape, dim):
    return lax.broadcasted_iota(jnp.int32, shape, dim)


def dot(a, b, ca, cb):
    return lax.dot_general(a, b, (((ca,), (cb,)), ((), ())), preferred_element_type=F32)


def halves(x):
    high = x.astype(BF)
    return high, (x - high.astype(F32)).astype(BF)


def call(body, out_shape, *args, scratch=(), fetch=False):
    specs = {"in_specs": [pl.BlockSpec(memory_space=pltpu.HBM)] * len(args)} if fetch else {}
    return pl.pallas_call(
        body,
        out_shape=out_shape,
        **specs,
        scratch_shapes=list(scratch),
        compiler_params=pltpu.CompilerParams(vmem_limit_bytes=48 << 20),
    )(*args)


def fetched(body, count):
    def kernel(*refs):
        given, out_ref, held, sems = refs[:count], refs[count], refs[count + 1 : -1], refs[-1]
        copies = [
            pltpu.make_async_copy(source, target, sems.at[place])
            for place, (source, target) in enumerate(zip(given, held))
        ]
        for copy in copies:
            copy.start()
        for copy in copies:
            copy.wait()
        body(*held, out_ref)

    return kernel


def held(args):
    return [pltpu.VMEM(a.shape, a.dtype) for a in args] + [pltpu.SemaphoreType.DMA((len(args),))]


def spread_body(k_ref, v_ref, g_ref, r_ref, w_ref, out_ref):
    width = k_ref.shape[0]
    head_size = k_ref.shape[1] // out_ref.shape[0]
    per = 128 // head_size
    eye = (iota((128, 128), 0) == iota((128, 128), 1)).astype(BF)
    routes = r_ref[...].astype(F32)
    weights = w_ref[...]
    high = weights.astype(BF).astype(F32)
    low = weights - high
    rows = iota((EXTRA, width), 0)
    common = jnp.zeros((EXTRA, width), F32)
    for place, line in enumerate(
        (routes[0:1], routes[1:2], high[0:1], high[1:2], low[0:1], low[1:2])
    ):
        common = jnp.where(rows == place + 1, line, common)
    decay = g_ref[...].astype(F32)
    for chunk in range(k_ref.shape[1] // 128):
        for base, ref in ((0, k_ref), (head_size, v_ref)):
            turned = dot(eye, ref[:, chunk * 128 : (chunk + 1) * 128], 1, 1).astype(BF)
            for part in range(per):
                out_ref[chunk * per + part, base : base + head_size, :] = turned[
                    part * head_size : (part + 1) * head_size, :
                ]
    for head in range(out_ref.shape[0]):
        out_ref[head, 2 * head_size : 2 * head_size + EXTRA, :] = jnp.where(
            rows == 0, decay[head : head + 1], common
        ).astype(BF)


def turn_body(q_ref, out_ref):
    head_size = out_ref.shape[1]
    per = 128 // head_size
    eye = (iota((128, 128), 0) == iota((128, 128), 1)).astype(BF)
    for chunk in range(q_ref.shape[1] // 128):
        turned = dot(eye, q_ref[:, chunk * 128 : (chunk + 1) * 128], 1, 1).astype(BF)
        for part in range(per):
            out_ref[chunk * per + part] = turned[part * head_size : (part + 1) * head_size, :]


def back_body(x_ref, out_ref):
    head_size = x_ref.shape[1]
    per = 128 // head_size
    eye = (iota((128, 128), 0) == iota((128, 128), 1)).astype(BF)
    for chunk in range(out_ref.shape[1] // 128):
        slab = x_ref[chunk * per : (chunk + 1) * per].reshape(128, 128)
        out_ref[:, chunk * 128 : (chunk + 1) * 128] = dot(eye, slab, 1, 1).astype(BF)


def tables(kv_ref):
    blocks, height, width = kv_ref.shape
    extra = kv_ref[:, height - EXTRA : height, :].astype(F32)
    ids = iota((blocks, ROWS, width), 1).astype(F32)
    member = (ids == extra[:, 1:2]) | (ids == extra[:, 2:3]) | (ids == float(MEMS))
    upper = (iota((width, width), 0) <= iota((width, width), 1)).astype(BF)
    decay = jnp.where(member, extra[:, 0:1], 0.0).reshape(blocks * ROWS, width).astype(BF)
    cumul = dot(decay, upper, 1, 0).reshape(blocks, ROWS, width)
    total = jnp.broadcast_to(cumul[:, :, width - 1 : width], cumul.shape)
    return extra, ids, member, cumul, total


def spread_out(kv_ref, block, reach, wide_ref, at):
    head_size = (kv_ref.shape[1] - EXTRA) // 2
    width = kv_ref.shape[2]
    keys = kv_ref[block, 0:head_size, :]
    values = kv_ref[block, head_size : 2 * head_size, :].astype(F32)
    for one in range(SETS):
        high, low = halves(values * reach[one : one + 1])
        rows = slice(one * head_size, (one + 1) * head_size)
        wide_ref[rows, at : at + width] = high
        wide_ref[rows, at + width : at + 2 * width] = low
    twice = jnp.concatenate([keys, keys], axis=0)
    return jnp.concatenate([twice, twice], axis=1)


TOGETHER = 2


def totals_body(pieces, kv_ref, out_ref, state_ref, reach_ref, wide_ref):
    blocks, height, width = kv_ref.shape
    head_size = (height - EXTRA) // 2
    _, _, member, cumul, total = tables(kv_ref)
    after = jnp.zeros((ROWS, width), F32)
    for block in reversed(range(blocks)):
        reach_ref[block] = jnp.where(
            member[block], jnp.exp(total[block] - cumul[block] + after), 0.0
        )
        after = after + total[block]
    state_ref[...] = jnp.zeros_like(state_ref)

    def step(turn, carry):
        keys = []
        for extra_block in range(TOGETHER):
            block = turn * TOGETHER + extra_block
            keys.append(
                spread_out(kv_ref, block, reach_ref[block], wide_ref, extra_block * 2 * width)
            )
        state_ref[...] += dot(wide_ref[...], jnp.concatenate(keys, axis=1), 1, 1)
        return carry

    lax.fori_loop(0, blocks // TOGETHER, step, 0)
    left = iota((8, width), 1) < head_size
    rows = iota((8, width), 0)
    parts = pieces // MEMS
    lines = head_size // 2 // parts
    plain = after.astype(BF).astype(F32)
    middle = (after - plain).astype(BF).astype(F32)
    rest = after - plain - middle
    for piece in range(pieces):
        one, part = piece // parts, piece % parts
        for base in range(0, lines, 8):
            start = one * head_size + part * 2 * lines + base
            out_ref[piece, base : base + 8, :] = jnp.where(
                left, state_ref[start : start + 8, :], state_ref[start + lines : start + lines + 8, :]
            ).astype(out_ref.dtype)
        start = MEMS * head_size + piece
        shared = jnp.where(
            left[0:1],
            state_ref[start : start + 1, :],
            state_ref[start + head_size // 2 : start + head_size // 2 + 1, :],
        )
        tail = jnp.where(rows == 0, shared, 0.0)
        for place, line in enumerate(
            (plain[one : one + 1], middle[one : one + 1], rest[one : one + 1],
             plain[MEMS : MEMS + 1], middle[MEMS : MEMS + 1], rest[MEMS : MEMS + 1])
        ):
            tail = jnp.where(rows == place + 1, line, tail)
        out_ref[piece, lines : lines + 8, :] = tail.astype(out_ref.dtype)


def prefix_body(x_ref, out_ref):
    peers, height, width = x_ref.shape
    lines = height - 8
    rows = iota((height, width), 0)
    before = jnp.zeros((height, width), F32)
    for peer in range(peers):
        out_ref[peer] = before.astype(out_ref.dtype)
        if peer < peers - 1:
            own = x_ref[peer].astype(F32)
            routed = own[lines + 1 : lines + 2] + own[lines + 2 : lines + 3] + own[lines + 3 : lines + 4]
            shared = own[lines + 4 : lines + 5] + own[lines + 5 : lines + 6] + own[lines + 6 : lines + 7]
            fade = jnp.exp(jnp.where(rows < lines, routed, shared))
            before = fade * before + own


def local_body(kv_ref, q_ref, out_ref, lift_ref, state_ref, pair_ref, wide_ref, reach_ref,
               read_ref, write_ref, fade_ref, near_ref):
    blocks, height, width = kv_ref.shape
    head_size = (height - EXTRA) // 2
    extra, ids, member, cumul, total = tables(kv_ref)
    share = (
        jnp.where(ids == extra[:, 1:2], extra[:, 3:4] + extra[:, 5:6], 0.0)
        + jnp.where(ids == extra[:, 2:3], extra[:, 4:5] + extra[:, 6:7], 0.0)
        + jnp.where(ids == float(MEMS), 1.0, 0.0)
    )
    middle = cumul[:, :, width // 2 - 1 : width // 2]
    write_ref[...] = jnp.where(member, jnp.exp(middle - cumul), 0.0)
    read_ref[...] = share * jnp.exp(cumul - middle)
    reach_ref[...] = jnp.where(member, jnp.exp(total - cumul), 0.0)
    fade_ref[...] = jnp.exp(total)
    near_ref[...] = share * jnp.exp(cumul)
    offset = jnp.zeros((ROWS, width), F32)
    for block in range(blocks):
        lift_ref[block] = share[block] * jnp.exp(cumul[block] + offset)
        offset = offset + total[block]
    state_ref[...] = jnp.zeros_like(state_ref)
    pair_ref[...] = jnp.zeros_like(pair_ref)

    def step(block, carry):
        keys = kv_ref[block, 0:head_size, :]
        values = kv_ref[block, head_size : 2 * head_size, :]
        queries = q_ref[block]
        pair = jnp.concatenate([queries, queries], axis=0)
        seen = dot(pair_ref[...], pair, 1, 0)
        write_high, write_low = halves(write_ref[block])
        read_high, read_low = halves(read_ref[block])
        factor = dot(
            jnp.concatenate([write_high, write_low, write_high], axis=0),
            jnp.concatenate([read_high, read_high, read_low], axis=0),
            0,
            0,
        )
        causal = iota((width, width), 0) <= iota((width, width), 1)
        scores = dot(keys, queries, 0, 0)
        high, low = halves(jnp.where(causal, scores * factor, 0.0))
        result = dot(
            jnp.concatenate([values, values], axis=1), jnp.concatenate([high, low], axis=0), 1, 0
        )
        lift = near_ref[block]
        fade = fade_ref[block]
        twice = spread_out(kv_ref, block, reach_ref[block], wide_ref, 0)
        fresh = dot(wide_ref[...], twice, 1, 1)
        left = iota((head_size, 2 * head_size), 1) < head_size
        for one in range(SETS):
            rows = slice(one * head_size, (one + 1) * head_size)
            result = result + lift[one : one + 1] * seen[rows]
            state = fade[one : one + 1] * state_ref[rows] + fresh[rows]
            state_ref[rows] = state
            high, low = halves(state)
            pair_ref[rows] = jnp.where(left, high, low)
        out_ref[block] = result
        return carry

    lax.fori_loop(0, blocks, step, 0)


def finish_body(before_ref, q_ref, local_ref, lift_ref, gain_ref, out_ref, all_ref, shared_ref):
    pieces = before_ref.shape[0]
    lines = before_ref.shape[1] - 8
    blocks, head_size, width = q_ref.shape
    parts = pieces // MEMS
    half = head_size // 2
    for piece in range(pieces):
        all_ref[piece * lines : (piece + 1) * lines, :] = before_ref[piece, 0:lines, :]
        shared_ref[piece : piece + 1, :] = before_ref[piece, lines : lines + 8, :].astype(F32)[0:1]
    routed = pieces * lines
    all_ref[routed : routed + half, :] = shared_ref[...].astype(BF)
    gain = gain_ref[...]

    def one_block(block):
        queries = q_ref[block]
        zero = jnp.zeros_like(queries)
        sides = jnp.concatenate(
            [jnp.concatenate([queries, zero], axis=1), jnp.concatenate([zero, queries], axis=1)],
            axis=0,
        )
        lift = lift_ref[block]
        seen = dot(all_ref[...], sides, 1, 0)
        line = lift[MEMS : MEMS + 1]
        near = line * seen[routed:, :width]
        far = line * seen[routed:, width:]
        add = [near, far]
        groups = []
        for part in range(parts):
            for side in range(2):
                total = None
                for one in range(MEMS):
                    start = (one * parts + part) * lines
                    term = lift[one : one + 1] * seen[
                        start : start + lines, side * width : (side + 1) * width
                    ]
                    total = term if total is None else total + term
                groups.append(total)
        combined = local_ref[block] + jnp.concatenate(groups, axis=0) + jnp.concatenate(add, axis=0)
        mean = jnp.sum(combined * combined, axis=0, keepdims=True) * (1.0 / head_size)
        out_ref[block] = (combined * lax.rsqrt(mean + 1e-06) * gain).astype(BF)

    def step(turn, carry):
        one_block(2 * turn)
        one_block(2 * turn + 1)
        return carry

    lax.fori_loop(0, blocks // 2, step, 0)


def shape(dims, dtype):
    return jax.ShapeDtypeStruct(dims, dtype)


def exchange(x, axis):
    return lax.all_to_all(x, axis, split_axis=0, concat_axis=0, tiled=True)


SEND = BF


def spread(keys, values, decay, routes, weights, heads):
    width = keys.shape[0]
    head_size = keys.shape[1] // heads
    args = (keys, values, decay.T, routes.T, weights.T)
    return call(
        fetched(spread_body, len(args)), shape((heads, 2 * head_size + EXTRA, width), BF), *args,
        scratch=held(args), fetch=True,
    )


def turn(queries, heads):
    return call(
        fetched(turn_body, 1), shape((heads, queries.shape[1] // heads, queries.shape[0]), BF),
        queries, scratch=held((queries,)), fetch=True,
    )


def totals(kv, pieces):
    head_size, width = (kv.shape[1] - EXTRA) // 2, kv.shape[2]
    lines = MEMS * head_size // 2 // pieces
    return call(
        functools.partial(totals_body, pieces), shape((pieces, lines + 8, width), SEND), kv,
        scratch=[
            pltpu.VMEM((SETS * head_size, width), F32),
            pltpu.VMEM((kv.shape[0], ROWS, width), F32),
            pltpu.VMEM((SETS * head_size, TOGETHER * 2 * width), BF),
        ],
    )


def prefix(x):
    return call(prefix_body, shape(x.shape, x.dtype), x)


def local(kv, q):
    blocks, head_size, width = q.shape
    return call(
        local_body,
        (shape((blocks, head_size, width), F32), shape((blocks, ROWS, width), F32)),
        kv, q,
        scratch=[
            pltpu.VMEM((SETS * head_size, width), F32),
            pltpu.VMEM((SETS * head_size, width), BF),
            pltpu.VMEM((SETS * head_size, 2 * width), BF),
        ]
        + [pltpu.VMEM((blocks, ROWS, width), F32)] * 5,
    )


def finish(before, q, inner, lift, gain):
    head_size, width = q.shape[1:]
    return call(
        finish_body, shape(q.shape, BF), before, q, inner, lift, gain,
        scratch=[
            pltpu.VMEM((SETS * head_size // 2, width), BF),
            pltpu.VMEM((head_size // 2, width), F32),
        ],
    )


def back(x, tokens, feats):
    return call(back_body, shape((tokens, feats), BF), x)


def on_device(queries, key_vectors, value_vectors, log_decay, routes, route_weight, out_gain):
    heads = lax.axis_size("mem")
    pieces = lax.axis_size("ctx")
    tokens, feats = queries.shape
    head_size = feats // heads
    kv = exchange(spread(key_vectors, value_vectors, log_decay, routes, route_weight, heads), "mem")
    turned = turn(queries, heads)
    q = exchange(turned, "mem")
    group = totals(kv, pieces)
    gathered = exchange(group, "ctx")
    inner, lift = local(kv, q)
    before = exchange(prefix(gathered), "ctx")
    mine = lax.dynamic_slice_in_dim(out_gain, lax.axis_index("mem") * head_size, head_size)
    gain = jnp.broadcast_to(mine[:, None], (head_size, tokens))
    done = exchange(finish(before, q, inner, lift, gain), "mem")
    return back(done, tokens, feats)


def solution(mesh):
    rows = P(("ctx", "mem"), None)

    return jax.shard_map(
        on_device,
        mesh=mesh,
        in_specs=(rows, rows, rows, rows, rows, rows, P()),
        out_specs=rows,
        check_vma=False,
    )
```

time: 128 us -> 111 us (0.87)
  Pallas kernels: 39.1 us -> 18.4 us
  waiting for transfers between devices: 20.5 us -> 23.7 us
    pallas_call x7, Pallas kernels: 39.1 us -> 18.4 us  [call(): pl.pallas_call(body, out_shape=out_shape, **specs, scratch_shapes=list(sc...]
    all_to_all x3, waiting for transfers between devices: 20.5 us -> 23.7 us  [exchange(): return lax.all_to_all(x, axis, split_axis=0, concat_axis=0, tiled=True)]
  transfers between devices with their start and end apart: 3 -> 3, of which waited for: 2 -> 3; matrix products, arithmetic and copies ran while one was open for 1% -> 1% of each run, Pallas kernels for 15% -> 9%
where the time goes in v2:
time: 111 us
  blocking collectives  45.5 us (41%)
  waiting for transfers between devices  23.7 us (21%)
  starting transfers between devices  19.1 us (17%)
  Pallas kernels  18.4 us (17%)
  local copies, waits for them, and re-layouts  4.11 us (4%)
    all_to_all x2, blocking collectives, exchange(): return lax.all_to_all(x, axis, split_axis=0, concat_axis=0, tiled=True)  45.5 us
    all_to_all x3, waiting for transfers between devices, exchange(): return lax.all_to_all(x, axis, split_axis=0, concat_axis=0, tiled=True)  23.7 us
    all_to_all x3, starting transfers between devices, exchange(): return lax.all_to_all(x, axis, split_axis=0, concat_axis=0, tiled=True)  19.1 us
    pallas_call x7, Pallas kernels, call(): pl.pallas_call(body, out_shape=out_shape, **specs, scratch_shapes=list(sc...  18.4 us
    unnamed x12, local copies, waits for them, and re-layouts  3.27 us
  transfers between devices with their start and end apart: 3, of which 3 were waited for; matrix products, arithmetic and copies ran while one was open for 1% of the time, Pallas kernels for 9%

profile of v2, /device:TPU:1, one launch (start us, length us, event | category | flops | bytes accessed | tf_op | source)
XLA Modules:
  0.0 110.8 jit_solution(12094767846164589095)
XLA Ops:
  0.0 0.0 copy-start.3
  0.0 0.0 copy-start.4
  0.0 0.7 copy-done.3
  0.7 0.0 copy-done.4
  0.7 0.0 copy-start
  0.7 0.9 copy-done
  1.6 0.0 copy-start.1
  1.6 0.9 copy-done.1
  2.6 0.0 copy-start.5
  2.6 0.7 copy-done.5
  3.3 0.6 shard_map.73
  3.9 30.5 %all_to_all.25.kv_ref = bf16[16,144,128]{2,1,0:T(8,128)(2,1)S(1)} all-to-all(bf16[16,144,128]{2,1,0:T(8,128)(2,1)S(1)} %shard_map.73), channel_id=1, replica_groups=mesh['ctx'=32,'mem'=16] {'mem'}, dimensions={0} | all-to-all | bytes 1179648 | tf_op jit(solution)/shard_map/all_to_all | solution.py:322
  34.4 4.8 %shard_map.74 = bf16[32,24,128]{2,1,0:T(8,128)(2,1)} custom-call(bf16[16,144,128]{2,1,0:T(8,128)(2,1)S(1)} %all_to_all.25.kv_ref), custom_call_target="tpu_custom_call" | custom-call | tf_op jit(solution)/shard_map/pallas_call | solution.py:34
  39.2 0.0 copy-start.2
  39.2 9.8 %all-to-all-start.1 = ((bf16[32,24,128]{2,1,0:T(8,128)(2,1)}), bf16[32,24,128]{2,1,0:T(8,128)(2,1)S(1)}, u32[]{:S(2)}, u32[]{:S(2)}) async-start(bf16[32,24,128]{2,1,0:T(8,128)(2,1)} %shard_map.74), calls=%async_computation.1 | async-start | bytes 393216 | tf_op jit(solution)/shard_map/all_to_all | solution.py:322
  49.0 0.0 copy-done.2
  49.0 1.0 shard_map.76
  50.0 9.5 %all-to-all-done.1.x_ref = bf16[32,24,128]{2,1,0:T(8,128)(2,1)S(1)} async-done(((bf16[32,24,128]{2,1,0:T(8,128)(2,1)}), bf16[32,24,128]{2,1,0:T(8,128)(2,1)S(1)}, u32[]{:S(2)}, u32[]{:S(2)}) %all-to-all-start.1) | async-done | bytes 196640 | tf_op jit(solution)/shard_map/all_to_all | solution.py:322
  59.5 5.5 %all-to-all-start.3 = ((bf16[16,64,128]{2,1,0:T(8,128)(2,1)}), bf16[16,64,128]{2,1,0:T(8,128)(2,1)S(1)}, u32[]{:S(2)}, u32[]{:S(2)}) async-start(bf16[16,64,128]{2,1,0:T(8,128)(2,1)} %shard_map.76), calls=%async_computation.3 | async-start | bytes 524288 | tf_op jit(solution)/shard_map/all_to_all | solution.py:322
  65.0 0.8 shard_map.75
  65.8 11.0 %all-to-all-done.3.q_ref = bf16[16,64,128]{2,1,0:T(8,128)(2,1)S(1)} async-done(((bf16[16,64,128]{2,1,0:T(8,128)(2,1)}), bf16[16,64,128]{2,1,0:T(8,128)(2,1)S(1)}, u32[]{:S(2)}, u32[]{:S(2)}) %all-to-all-start.3) | async-done | bytes 262176 | tf_op jit(solution)/shard_map/all_to_all | solution.py:322
  76.7 3.9 %all-to-all-start.2 = ((bf16[32,24,128]{2,1,0:T(8,128)(2,1)}), bf16[32,24,128]{2,1,0:T(8,128)(2,1)S(1)}, u32[]{:S(2)}, u32[]{:S(2)}) async-start(bf16[32,24,128]{2,1,0:T(8,128)(2,1)} %shard_map.75), calls=%async_computation.2 | async-start | bytes 393216 | tf_op jit(solution)/shard_map/all_to_all | solution.py:322
  80.6 0.8 dynamic_slice.3
  81.4 7.6 %shard_map.77 = (f32[16,64,128]{2,1,0:T(8,128)S(1)}, f32[16,24,128]{2,1,0:T(8,128)S(1)}) custom-call(bf16[16,144,128]{2,1,0:T(8,128)(2,1)S(1)} %all_to_all.25.kv_ref, bf16[16,64,128]{2,1,0:T(8,128)(2,1)S(1)} %all-to-all-done.3.q_ref), custom_call_target="tpu_custom_call" | custom-call | tf_op jit(solution)/shard_map/pallas_call | solution.py:34
  89.0 3.2 %all-to-all-done.2.before_ref = bf16[32,24,128]{2,1,0:T(8,128)(2,1)S(1)} async-done(((bf16[32,24,128]{2,1,0:T(8,128)(2,1)}), bf16[32,24,128]{2,1,0:T(8,128)(2,1)S(1)}, u32[]{:S(2)}, u32[]{:S(2)}) %all-to-all-start.2) | async-done | bytes 196640 | tf_op jit(solution)/shard_map/all_to_all | solution.py:322
  92.2 0.1 broadcast_in_dim.2.gain_ref
  92.3 2.6 %shard_map.78 = bf16[16,64,128]{2,1,0:T(8,128)(2,1)S(1)} custom-call(bf16[32,24,128]{2,1,0:T(8,128)(2,1)S(1)} %all-to-all-done.2.before_ref, bf16[16,64,128]{2,1,0:T(8,128)(2,1)S(1)} %all-to-all-done.3.q_ref, f32[16,64,128]{2,1,0:T(8,128)S(1)} %get-tuple-element.7.local_ref, f32[16,24,128]{2,1,0:T(8,128)S(1)} %get-tuple-element.8.lift_ref, ...), custom_call_target="tpu_custom_call" | custom-call | tf_op jit(solution)/shard_map/pallas_call | solution.py:34
  94.9 14.9 %all_to_all.26.x_ref = bf16[16,64,128]{2,1,0:T(8,128)(2,1)S(1)} all-to-all(bf16[16,64,128]{2,1,0:T(8,128)(2,1)S(1)} %shard_map.78), channel_id=1, replica_groups=mesh['ctx'=32,'mem'=16] {'mem'}, dimensions={0} | all-to-all | bytes 524288 | tf_op jit(solution)/shard_map/all_to_all | solution.py:322
  109.8 1.0 shard_map.79
Async XLA Ops:
  0.0 0.7 copy-start.3
  0.0 0.7 copy-start.4
  0.7 0.9 copy-start
  1.6 0.9 copy-start.1
  2.6 0.7 copy-start.5
  39.2 9.8 %copy-start.2 = (bf16[128,1024]{1,0:T(8,128)(2,1)S(1)}, bf16[128,1024]{1,0:T(8,128)(2,1)}, u32[]{:S(2)}) copy-start(bf16[128,1024]{1,0:T(8,128)(2,1)} %refs_0_.3) | copy-start | bytes 786436
  39.2 20.4 %all-to-all-start.1 = ((bf16[32,24,128]{2,1,0:T(8,128)(2,1)}), bf16[32,24,128]{2,1,0:T(8,128)(2,1)S(1)}, u32[]{:S(2)}, u32[]{:S(2)}) async-start(bf16[32,24,128]{2,1,0:T(8,128)(2,1)} %shard_map.74), calls=%async_computation.1 | async-start | bytes 393216 | tf_op jit(solution)/shard_map/all_to_all | solution.py:322
  59.5 17.2 %all-to-all-start.3 = ((bf16[16,64,128]{2,1,0:T(8,128)(2,1)}), bf16[16,64,128]{2,1,0:T(8,128)(2,1)S(1)}, u32[]{:S(2)}, u32[]{:S(2)}) async-start(bf16[16,64,128]{2,1,0:T(8,128)(2,1)} %shard_map.76), calls=%async_computation.3 | async-start | bytes 524288 | tf_op jit(solution)/shard_map/all_to_all | solution.py:322
  76.7 15.5 %all-to-all-start.2 = ((bf16[32,24,128]{2,1,0:T(8,128)(2,1)}), bf16[32,24,128]{2,1,0:T(8,128)(2,1)S(1)}, u32[]{:S(2)}, u32[]{:S(2)}) async-start(bf16[32,24,128]{2,1,0:T(8,128)(2,1)} %shard_map.75), calls=%async_computation.2 | async-start | bytes 393216 | tf_op jit(solution)/shard_map/all_to_all | solution.py:322
